TPU v7x, 256 devices: a whole 4x4x8 slice. The times are simulated.
256 devices in a mesh: ctx: 16 (over z, core), exp: 16 (over x, y).
Axes of the slice: x: 4, y: 4, z: 8, core: 2. Of those that a mesh axis runs over, the one named last changes fastest.
Arguments:
- query_input: bfloat16 [2048, 8192], P('ctx', 'exp'), may hold values from -6 to 6
- key_input: bfloat16 [2048, 8192], P('ctx', 'exp'), may hold values from -6 to 6
- value_input: bfloat16 [2048, 8192], P('ctx', 'exp'), may hold values from -6 to 6
- gate_logits: float32 [2, 2048, 64], P(None, 'ctx', 'exp'), may hold values from -6 to 6
- comp_weight: float32 [2, 32, 64], P(None, None, 'exp'), may hold values from -6 to 6
- out_proj: bfloat16 [8192, 7168], P('exp', 'ctx'), may hold values from -0.0625 to 0.0625
- residual_in: bfloat16 [2048, 7168], P(('ctx', 'exp')), may hold values from -3 to 3
- ffn_gain: float32 [7168], replicated, may hold values from 0.25 to 1.75
- expert_ids: int32 [2048, 2], P(('ctx', 'exp')), may hold values from 0 to 15, all different within a row; in each aligned block of 8 rows (0 to 7, 8 to 15, ...) at most 2 rows name the same one
- route_gates: float32 [2048, 2], P(('ctx', 'exp')), may hold values from 0.2 to 1
- expert_gate: bfloat16 [16, 7168, 2048], P('exp', None, 'ctx'), may hold values from -0.0625 to 0.0625
- expert_up: bfloat16 [16, 7168, 2048], P('exp', None, 'ctx'), may hold values from -0.0625 to 0.0625
- expert_down: bfloat16 [16, 2048, 7168], P('exp', 'ctx'), may hold values from -0.125 to 0.125
Outputs:
- layer_out: bfloat16 [2048, 7168], P(('ctx', 'exp'))
Inputs may be any that keep to these rules, and one draw needn't show every extreme that they name: `expert_ids`: each token names 2 different experts. In every aligned block of 8 consecutive tokens no expert is named more than 2 times, a bound that some block reaches.
All inputs are finite; a program needn't handle non-finite values.
Results may differ from a plain program's by a relative error of at most 0.0085.
Values may be sent and summed in bfloat16 or wider, within the bound.
A program may use at most 128 MiB of HBM per device.

v0:
```python
import math
import jax
import jax.numpy as jnp
from jax import lax
from jax.sharding import PartitionSpec as P

WINDOW = 512
score_gain = 2.0
norm_eps = 1e-06


def passed_along(block, axis, distance):
    devices = range(lax.axis_size(axis))
    route = [(i - distance, i) for i in devices if i - distance in devices]
    return lax.ppermute(block, axis, route)


def head_norm(matrix, head_width):
    row_count = matrix.shape[0]
    shaped = matrix.reshape(row_count, -1, head_width).astype(jnp.float32)
    scaled = shaped * lax.rsqrt(jnp.mean(shaped * shaped, axis=2, keepdims=True) + norm_eps)
    return scaled.reshape(row_count, -1)


def compress(extended, position_weights, head_width):
    stride_len = position_weights.shape[0] // 2
    head_count = position_weights.shape[1]
    blocks = extended.reshape(-1, stride_len, head_count, head_width).astype(jnp.float32)
    first_half = jnp.einsum(
        "nshd,sh->nhd", blocks[:-1], position_weights[:stride_len], precision=lax.Precision.HIGHEST
    )
    second_half = jnp.einsum(
        "nshd,sh->nhd", blocks[1:], position_weights[stride_len:], precision=lax.Precision.HIGHEST
    )
    return (first_half + second_half).reshape(blocks.shape[0] - 1, head_count * head_width)


def local(
    query_input,
    key_input,
    value_input,
    gate_logits,
    comp_weight,
    out_proj,
    residual_in,
    ffn_gain,
    expert_ids,
    route_gates,
    expert_gate,
    expert_up,
    expert_down,
):
    row_count = query_input.shape[0]
    head_count = comp_weight.shape[2]
    head_width = query_input.shape[1] // head_count
    block_len = comp_weight.shape[1]
    stride_len = block_len // 2
    exp_count = lax.axis_size("exp")
    ctx_index = lax.axis_index("ctx")
    scale = score_gain / math.sqrt(head_width)
    query_norm = head_norm(query_input, head_width).astype(jnp.bfloat16)
    key_norm = head_norm(key_input, head_width).astype(jnp.bfloat16)
    next_keys, next_values = passed_along(
        (key_input[:stride_len], value_input[:stride_len]), "ctx", -1
    )
    comp_keys = head_norm(
        compress(jnp.concatenate([key_input, next_keys], 0), comp_weight[0], head_width), head_width
    ).astype(jnp.bfloat16)
    comp_values = compress(
        jnp.concatenate([value_input, next_values], 0), comp_weight[1], head_width
    ).astype(jnp.bfloat16)
    query_pos = ctx_index * row_count + jnp.arange(row_count, dtype=jnp.int32)
    query_heads = query_norm.reshape(row_count, head_count, head_width)
    part_keys = lax.all_gather(comp_keys, "ctx", axis=0, tiled=True)
    part_values = lax.all_gather(comp_values, "ctx", axis=0, tiled=True)
    part_count = part_keys.shape[0]
    scores = jnp.einsum(
        "thd,nhd->htn",
        query_heads,
        part_keys.reshape(part_count, head_count, head_width),
        preferred_element_type=jnp.float32,
    )
    block_end = jnp.arange(part_count, dtype=jnp.int32) * stride_len + block_len - 1
    visible = block_end[None, :] <= query_pos[:, None]
    weights = jnp.where(visible[None], jnp.exp(scale * scores), 0.0)
    running_total = jnp.sum(weights, axis=2).T
    collected = jnp.einsum(
        "htn,nhd->thd",
        weights.astype(jnp.bfloat16),
        part_values.reshape(part_count, head_count, head_width),
        preferred_element_type=jnp.float32,
    )
    cmp_sum = collected.reshape(row_count, -1)
    no_block = (query_pos < block_len - 1).astype(jnp.float32)
    cmp_out = (
        cmp_sum.reshape(row_count, head_count, head_width)
        / (running_total + no_block[:, None])[:, :, None]
    )
    shift_count = max(1, WINDOW // row_count)
    earlier_keys = []
    earlier_values = []
    for distance in range(shift_count, 0, -1):
        moved_keys, moved_values = passed_along((key_norm, value_input), "ctx", distance)
        earlier_keys.append(moved_keys)
        earlier_values.append(moved_values)
    near_keys = jnp.concatenate(earlier_keys + [key_norm], 0)
    near_values = jnp.concatenate(earlier_values + [value_input], 0)
    key_pos = ctx_index * row_count - WINDOW + jnp.arange(near_keys.shape[0], dtype=jnp.int32)
    near_scores = jnp.einsum(
        "thd,shd->hts",
        query_heads,
        near_keys.reshape(-1, head_count, head_width),
        preferred_element_type=jnp.float32,
    )
    inside = (
        (key_pos[None, :] <= query_pos[:, None])
        & (key_pos[None, :] > query_pos[:, None] - WINDOW)
        & (key_pos[None, :] >= 0)
    )
    near_weights = jnp.where(inside[None], jnp.exp(scale * near_scores), 0.0)
    win_total = jnp.sum(near_weights, axis=2).T
    win_sum = jnp.einsum(
        "hts,shd->thd",
        near_weights.astype(jnp.bfloat16),
        near_values.reshape(-1, head_count, head_width),
        preferred_element_type=jnp.float32,
    )
    win_out = win_sum / win_total[:, :, None]
    branch_gates = jax.nn.sigmoid(gate_logits)
    attended = (
        (branch_gates[0][:, :, None] * cmp_out + branch_gates[1][:, :, None] * win_out)
        .reshape(row_count, -1)
        .astype(jnp.bfloat16)
    )
    token_share = row_count // exp_count
    partial_sum = jnp.dot(
        attended,
        lax.all_gather(out_proj, "ctx", axis=1, tiled=True),
        preferred_element_type=jnp.float32,
    )
    projected = lax.psum_scatter(partial_sum, "exp", scatter_dimension=0, tiled=True)
    hidden_state = residual_in.astype(jnp.float32) + projected
    mean_square = jnp.mean(hidden_state * hidden_state, axis=1, keepdims=True)
    normed = (hidden_state * lax.rsqrt(mean_square + norm_eps) * ffn_gain).astype(jnp.bfloat16)
    model_width = normed.shape[1]
    top_count = expert_ids.shape[1]
    capacity = max(2, 2 * token_share * top_count // exp_count)
    flat_ids = expert_ids.reshape(-1)
    chosen = (flat_ids[:, None] == jnp.arange(exp_count, dtype=jnp.int32)[None, :]).astype(
        jnp.int32
    )
    slots = jnp.sum((jnp.cumsum(chosen, axis=0) - chosen) * chosen, axis=1)
    targets = (flat_ids * capacity + slots).reshape(token_share, top_count)
    slot_range = jnp.arange(exp_count * capacity, dtype=jnp.int32)
    dispatch_map = jnp.sum(
        (slot_range[:, None, None] == targets[None, :, :]).astype(jnp.float32), axis=2
    ).astype(jnp.bfloat16)
    outgoing = (
        jnp.dot(dispatch_map, normed, preferred_element_type=jnp.float32)
        .astype(jnp.bfloat16)
        .reshape(exp_count, capacity, model_width)
    )
    arrived = lax.all_to_all(outgoing, "exp", split_axis=0, concat_axis=0, tiled=True)
    gate_cols = expert_gate[0]
    up_cols = expert_up[0]
    down_rows = expert_down[0]
    portion = lax.all_gather(arrived, "ctx", axis=0, tiled=True)
    flat_rows = portion.reshape(-1, model_width)
    gate_part = jnp.dot(flat_rows, gate_cols, preferred_element_type=jnp.float32)
    up_part = jnp.dot(flat_rows, up_cols, preferred_element_type=jnp.float32)
    activated = (jax.nn.silu(gate_part) * up_part).astype(jnp.bfloat16)
    partial_out = jnp.dot(activated, down_rows, preferred_element_type=jnp.float32).reshape(
        portion.shape
    )
    finished = lax.psum_scatter(
        partial_out.astype(jnp.bfloat16), "ctx", scatter_dimension=0, tiled=True
    )
    returned = lax.all_to_all(finished, "exp", split_axis=0, concat_axis=0, tiled=True).reshape(
        -1, model_width
    )
    combine_map = jnp.sum(
        jnp.where(slot_range[None, None, :] == targets[:, :, None], route_gates[:, :, None], 0.0),
        axis=1,
    )
    moe_out = jnp.dot(combine_map, returned.astype(jnp.float32), precision=lax.Precision.HIGHEST)
    return (hidden_state + moe_out).astype(jnp.bfloat16)


def solution(mesh):
    in_specs = (
        P("ctx", "exp"),
        P("ctx", "exp"),
        P("ctx", "exp"),
        P(None, "ctx", "exp"),
        P(None, None, "exp"),
        P("exp", "ctx"),
        P(("ctx", "exp"), None),
        P(),
        P(("ctx", "exp"), None),
        P(("ctx", "exp"), None),
        P("exp", None, "ctx"),
        P("exp", None, "ctx"),
        P("exp", "ctx", None),
    )
    out_specs = P(("ctx", "exp"), None)
    return jax.shard_map(local, mesh=mesh, in_specs=in_specs, out_specs=out_specs, check_vma=False)
```

profile of v0, /device:TPU:8, one launch (start us, length us, event | category | flops | bytes accessed | tf_op | source)
XLA Modules:
  0.0 412.8 jit_solution(15140837322775450915)
XLA Ops:
  8.4 5.2 %collective-permute-start.6 = (bf16[128,512]{0,1:T(8,128)(2,1)S(1)}, bf16[128,512]{0,1:T(8,128)(2,1)S(1)}, u32[]{:S(2)}, u32[]{:S(2)}) collective-permute-start(bf16[128,512]{0,1:T(8,128)(2,1)S(1)} %fusion.24), channel_id=1, source_target_pairs={{0,64},{16,80},{32,96},{48,112},{64,128},{80,144},{96,160},{112,17... | collective-permute-start | bytes 393224 | tf_op jit(solution)/shard_map/ppermute | solution.py:15
  13.6 3.0 collective-permute-start.7
  16.6 5.0 %collective-permute-start.8 = (bf16[128,512]{0,1:T(8,128)(2,1)S(1)}, bf16[128,512]{0,1:T(8,128)(2,1)S(1)}, u32[]{:S(2)}, u32[]{:S(2)}) collective-permute-start(bf16[128,512]{0,1:T(8,128)(2,1)S(1)} %fusion.24), channel_id=1, source_target_pairs={{0,32},{16,48},{32,64},{48,80},{64,96},{80,112},{96,128},{112,144}... | collective-permute-start | bytes 393224 | tf_op jit(solution)/shard_map/ppermute | solution.py:15
  21.7 3.4 collective-permute-start.2
  25.1 1.3 slice.74
  26.4 1.3 collective-permute-start.1
  27.7 1.6 slice.71
  32.8 1.4 fusion.49
  38.0 3.6 collective-permute-start.3
  42.1 18.2 %all_gather.13 = bf16[128,512]{1,0:T(8,128)(2,1)S(1)} all-gather(bf16[8,512]{1,0:T(8,128)(2,1)S(1)} %fusion.45), channel_id=1, replica_groups=mesh['ctx'=16,'exp'=16] {'ctx'}, dimensions={0}, use_global_device_ids=true | all-gather | bytes 139264 | tf_op jit(solution)/shard_map/all_gather | solution.py:74
  61.3 2.9 collective-permute-start.4
  64.2 2.0 collective-permute-start.5
  66.2 4.5 %collective-permute-done.4 = bf16[128,512]{1,0:T(8,128)(2,1)S(1)} collective-permute-done((bf16[128,512]{1,0:T(8,128)(2,1)S(1)}, bf16[128,512]{1,0:T(8,128)(2,1)S(1)}, u32[]{:S(2)}, u32[]{:S(2)}) %collective-permute-start.4) | collective-permute-done | bytes 131104 | tf_op jit(solution)/shard_map/ppermute | solution.py:15
  70.8 1.9 collective-permute-start.9
  72.7 1.3 collective-permute-start
  74.1 4.0 collective-permute-done
  79.8 19.0 %all_gather.12 = bf16[128,512]{1,0:T(8,128)(2,1)S(1)} all-gather(bf16[8,512]{1,0:T(8,128)(2,1)S(1)} %fusion.44), channel_id=1, replica_groups=mesh['ctx'=16,'exp'=16] {'ctx'}, dimensions={0}, use_global_device_ids=true | all-gather | bytes 139264 | tf_op jit(solution)/shard_map/all_gather | solution.py:75
  100.0 1.6 constant_dynamic-update-slice_fusion.6
  102.3 1.7 fusion.50
  104.6 7.5 %fusion.52 = f32[128,7168]{1,0:T(8,128)} fusion(bf16[128,512]{0,1:T(8,128)(2,1)S(1)} %bitcast.126, bf16[512,7168]{0,1:T(8,128)(2,1)} %all-gather.3.cloned.1.call-done), kind=kOutput, calls=%fused_computation.101 | convolution fusion | flops 939524096 | bytes 11141120 | tf_op jit(solution)/shard_map/dot_general | solution.py:136
  114.8 107.4 %all-reduce.3.cloned.1.call-done = f32[128,7168]{1,0:T(8,128)} async-done(((f32[128,7168]{1,0:T(8,128)}), f32[128,7168]{1,0:T(8,128)}) %all-reduce.3.cloned.1.call-update) | async-done | bytes 3670032
  224.7 15.1 %all_to_all.10 = bf16[16,2,7168]{2,1,0:T(2,128)(2,1)} all-to-all(bf16[16,2,7168]{2,1,0:T(2,128)(2,1)S(1)} %reshape.231), channel_id=1, replica_groups=mesh['ctx'=16,'exp'=16] {'exp'}, dimensions={0} | all-to-all | bytes 917504 | tf_op jit(solution)/shard_map/all_to_all | solution.py:163
  240.1 49.7 %all-gather.5.cloned.1.call-done = bf16[256,2,7168]{2,1,0:T(2,128)(2,1)} async-done(((bf16[16,2,7168]{2,1,0:T(2,128)(2,1)}), bf16[256,2,7168]{2,1,0:T(2,128)(2,1)}) %all-gather.5.cloned.1.call-update) | async-done | bytes 7340048 | tf_op jit(solution)/shard_map/all_gather | solution.py:167
  289.8 15.4 %reshape.232 = bf16[512,7168]{1,0:T(8,128)(2,1)} reshape(bf16[256,2,7168]{2,1,0:T(2,128)(2,1)} %all-gather.5.cloned.1.call-done) | data formatting | bytes 14680064 | tf_op jit(solution)/shard_map/reshape | solution.py:168
  305.2 5.8 %fusion.4 = f32[512,128]{1,0:T(8,128)S(1)} fusion(bf16[512,7168]{1,0:T(8,128)(2,1)} %reshape.232, bf16[1,7168,128]{2,1,0:T(8,128)(2,1)} %param.23), kind=kOutput, calls=%fused_computation.7 | convolution fusion | flops 939524096 | bytes 9437184 | tf_op jit(solution)/shard_map/dot_general | solution.py:169
  311.4 2.1 fusion.19
  313.4 5.0 %convolution_convert_fusion = bf16[256,2,7168]{2,0,1:T(8,128)(2,1)} fusion(bf16[1,128,7168]{2,1,0:T(8,128)(2,1)S(1)} %copy-done, bf16[256,2,128]{2,1,0:T(2,128)(2,1)S(1)} %bitcast.127), kind=kOutput, calls=%fused_computation | convolution fusion | flops 943194112 | bytes 9306112 | tf_op jit(solution)/shard_map/dot_general | solution.py:172
  318.5 67.8 %reduce-scatter.2.cloned.1.call-done = bf16[16,2,7168]{2,0,1:T(8,128)(2,1)} async-done(((bf16[256,2,7168]{2,0,1:T(8,128)(2,1)}), bf16[16,2,7168]{2,0,1:T(8,128)(2,1)}) %reduce-scatter.2.cloned.1.call-update) | async-done | bytes 458768 | tf_op jit(solution)/shard_map/reduce_scatter | solution.py:175
  386.3 2.3 copy.99
  388.6 7.3 %all-to-all-start.1 = ((bf16[16,2,7168]{2,1,0:T(2,128)(2,1)}), bf16[16,2,7168]{2,1,0:T(2,128)(2,1)S(1)}, u32[]{:S(2)}, u32[]{:S(2)}) async-start(bf16[16,2,7168]{2,1,0:T(2,128)(2,1)} %copy.99), calls=%async_computation.2 | async-start | bytes 917504 | tf_op jit(solution)/shard_map/all_to_all | solution.py:178
  395.9 8.3 %all-to-all-done.1 = bf16[16,2,7168]{2,1,0:T(2,128)(2,1)S(1)} async-done(((bf16[16,2,7168]{2,1,0:T(2,128)(2,1)}), bf16[16,2,7168]{2,1,0:T(2,128)(2,1)S(1)}, u32[]{:S(2)}, u32[]{:S(2)}) %all-to-all-start.1) | async-done | bytes 458784 | tf_op jit(solution)/shard_map/all_to_all | solution.py:178
  404.4 1.9 fusion
  (114 shorter events, 20.1 us)
Async XLA Ops:
  6.5 306.9 %copy-start = (bf16[1,128,7168]{2,1,0:T(8,128)(2,1)S(1)}, bf16[1,128,7168]{2,1,0:T(8,128)(2,1)}, u32[]{:S(2)}) copy-start(bf16[1,128,7168]{2,1,0:T(8,128)(2,1)} %param.25) | copy-start | bytes 5505028
  6.5 35.1 %copy-start.2 = (bf16[128,512]{1,0:T(8,128)(2,1)S(1)}, bf16[128,512]{1,0:T(8,128)(2,1)}, u32[]{:S(2)}) copy-start(bf16[128,512]{1,0:T(8,128)(2,1)} %param.14) | copy-start | bytes 393220
  6.5 30.8 %copy-start.4 = (bf16[128,512]{1,0:T(8,128)(2,1)S(1)}, bf16[128,512]{1,0:T(8,128)(2,1)}, u32[]{:S(2)}) copy-start(bf16[128,512]{1,0:T(8,128)(2,1)} %param.15) | copy-start | bytes 393220
  6.5 30.7 %copy-start.5 = (bf16[128,512]{1,0:T(8,128)(2,1)S(1)}, bf16[128,512]{1,0:T(8,128)(2,1)}, u32[]{:S(2)}) copy-start(bf16[128,512]{1,0:T(8,128)(2,1)} %param.13) | copy-start | bytes 393220
  6.5 98.1 %all-gather.3.cloned.1.call-start = ((), (), s32[]{:S(2)}) async-start(), calls=%async_computation.3 | async-start | bytes 7798784 | tf_op jit(solution)/shard_map/all_gather | solution.py:138
  7.3 214.9 %all-reduce.3.cloned.1.call-start = ((), (), s32[]{:S(2)}) async-start(), calls=%async_computation.6 | async-start | bytes 7340032
  8.4 71.3 %collective-permute-start.6 = (bf16[128,512]{0,1:T(8,128)(2,1)S(1)}, bf16[128,512]{0,1:T(8,128)(2,1)S(1)}, u32[]{:S(2)}, u32[]{:S(2)}) collective-permute-start(bf16[128,512]{0,1:T(8,128)(2,1)S(1)} %fusion.24), channel_id=1, source_target_pairs={{0,64},{16,80},{32,96},{48,112},{64,128},{80,144},{96,160},{112,17... | collective-permute-start | bytes 393224 | tf_op jit(solution)/shard_map/ppermute | solution.py:15
  13.6 66.2 %collective-permute-start.7 = (bf16[128,512]{0,1:T(8,128)(2,1)S(1)}, bf16[128,512]{0,1:T(8,128)(2,1)S(1)}, u32[]{:S(2)}, u32[]{:S(2)}) collective-permute-start(bf16[128,512]{0,1:T(8,128)(2,1)S(1)} %fusion.24), channel_id=1, source_target_pairs={{0,48},{16,64},{32,80},{48,96},{64,112},{80,128},{96,144},{112,160... | collective-permute-start | bytes 393224 | tf_op jit(solution)/shard_map/ppermute | solution.py:15
  16.6 82.7 %collective-permute-start.8 = (bf16[128,512]{0,1:T(8,128)(2,1)S(1)}, bf16[128,512]{0,1:T(8,128)(2,1)S(1)}, u32[]{:S(2)}, u32[]{:S(2)}) collective-permute-start(bf16[128,512]{0,1:T(8,128)(2,1)S(1)} %fusion.24), channel_id=1, source_target_pairs={{0,32},{16,48},{32,64},{48,80},{64,96},{80,112},{96,128},{112,144}... | collective-permute-start | bytes 393224 | tf_op jit(solution)/shard_map/ppermute | solution.py:15
  21.7 39.6 %collective-permute-start.2 = (bf16[128,512]{1,0:T(8,128)(2,1)}, bf16[128,512]{1,0:T(8,128)(2,1)S(1)}, u32[]{:S(2)}, u32[]{:S(2)}) collective-permute-start(bf16[128,512]{1,0:T(8,128)(2,1)} %param.15), channel_id=1, source_target_pairs={{0,64},{16,80},{32,96},{48,112},{64,128},{80,144},{96,160},{112,17... | collective-permute-start | bytes 393224 | tf_op jit(solution)/shard_map/ppermute | solution.py:15
  26.4 11.6 %collective-permute-start.1 = (bf16[16,512]{1,0:T(8,128)(2,1)}, bf16[16,512]{1,0:T(8,128)(2,1)S(1)}, u32[]{:S(2)}, u32[]{:S(2)}) collective-permute-start(bf16[16,512]{1,0:T(8,128)(2,1)} %slice.74), channel_id=1, source_target_pairs={{16,0},{32,16},{48,32},{64,48},{80,64},{96,80},{112,96},{128,112},... | collective-permute-start | bytes 49160 | tf_op jit(solution)/shard_map/ppermute | solution.py:15
  37.3 24.0 %copy-start.6 = (bf16[16,4,8,128]{3,2,1,0:T(8,128)(2,1)}, bf16[16,4,8,128]{3,2,1,0:T(8,128)(2,1)S(1)}, u32[]{:S(2)}) copy-start(bf16[16,4,8,128]{3,2,1,0:T(8,128)(2,1)S(1)} %fusion.25) | copy-start | bytes 393220
  38.0 26.2 %collective-permute-start.3 = (bf16[128,512]{1,0:T(8,128)(2,1)S(1)}, bf16[128,512]{1,0:T(8,128)(2,1)S(1)}, u32[]{:S(2)}, u32[]{:S(2)}) collective-permute-start(bf16[128,512]{1,0:T(8,128)(2,1)S(1)} %copy-done.4), channel_id=1, source_target_pairs={{0,48},{16,64},{32,80},{48,96},{64,112},{80,128},{96,144},{112,160... | collective-permute-start | bytes 393224 | tf_op jit(solution)/shard_map/ppermute | solution.py:15
  61.3 42.7 %copy-start.10 = (f32[128,4]{0,1:T(4,128)S(1)}, f32[128,4]{0,1:T(4,128)}, u32[]{:S(2)}) copy-start(f32[128,4]{0,1:T(4,128)} %get-tuple-element.8) | copy-start | bytes 6148
  61.3 9.5 %collective-permute-start.4 = (bf16[128,512]{1,0:T(8,128)(2,1)S(1)}, bf16[128,512]{1,0:T(8,128)(2,1)S(1)}, u32[]{:S(2)}, u32[]{:S(2)}) collective-permute-start(bf16[128,512]{1,0:T(8,128)(2,1)S(1)} %copy-done.4), channel_id=1, source_target_pairs={{0,32},{16,48},{32,64},{48,80},{64,96},{80,112},{96,128},{112,144}... | collective-permute-start | bytes 393224 | tf_op jit(solution)/shard_map/ppermute | solution.py:15
  64.2 8.5 %collective-permute-start.5 = (bf16[128,512]{1,0:T(8,128)(2,1)S(1)}, bf16[128,512]{1,0:T(8,128)(2,1)S(1)}, u32[]{:S(2)}, u32[]{:S(2)}) collective-permute-start(bf16[128,512]{1,0:T(8,128)(2,1)S(1)} %copy-done.4), channel_id=1, source_target_pairs={{0,16},{16,32},{32,48},{48,64},{64,80},{80,96},{96,112},{112,128},... | collective-permute-start | bytes 393224 | tf_op jit(solution)/shard_map/ppermute | solution.py:15
  70.8 29.3 %collective-permute-start.9 = (bf16[128,512]{0,1:T(8,128)(2,1)S(1)}, bf16[128,512]{0,1:T(8,128)(2,1)}, u32[]{:S(2)}, u32[]{:S(2)}) collective-permute-start(bf16[128,512]{0,1:T(8,128)(2,1)S(1)} %fusion.24), channel_id=1, source_target_pairs={{0,16},{16,32},{32,48},{48,64},{64,80},{80,96},{96,112},{112,128},... | collective-permute-start | bytes 393224 | tf_op jit(solution)/shard_map/ppermute | solution.py:15
  72.7 5.4 %collective-permute-start = (bf16[16,512]{1,0:T(8,128)(2,1)}, bf16[16,512]{1,0:T(8,128)(2,1)S(1)}, u32[]{:S(2)}, u32[]{:S(2)}) collective-permute-start(bf16[16,512]{1,0:T(8,128)(2,1)} %slice.66), channel_id=1, source_target_pairs={{16,0},{32,16},{48,32},{64,48},{80,64},{96,80},{112,96},{128,112},... | collective-permute-start | bytes 49160 | tf_op jit(solution)/shard_map/ppermute | solution.py:15
  79.8 24.6 %copy-start.9 = (f32[128,4]{0,1:T(4,128)S(1)}, f32[128,4]{0,1:T(4,128)}, u32[]{:S(2)}) copy-start(f32[128,4]{0,1:T(4,128)} %get-tuple-element.7) | copy-start | bytes 6148
  79.8 19.1 %copy-start.8 = (bf16[640,512]{0,1:T(8,128)(2,1)}, bf16[640,512]{0,1:T(8,128)(2,1)S(1)}, u32[]{:S(2)}) copy-start(bf16[640,512]{0,1:T(8,128)(2,1)S(1)} %constant_dynamic-update-slice_fusion.8) | copy-start | bytes 1966084
  99.2 5.2 %copy-start.15 = (bf16[4,128,128]{1,2,0:T(8,128)(2,1)S(1)}, bf16[4,128,128]{1,2,0:T(8,128)(2,1)}, u32[]{:S(2)}) copy-start(bf16[4,128,128]{1,2,0:T(8,128)(2,1)} %get-tuple-element.16) | copy-start | bytes 393220
  112.1 0.7 copy-start.11
  112.1 1.3 copy-start.14
  112.1 110.0 %copy-start.3 = (bf16[8,7168]{1,0:T(8,128)(2,1)S(1)}, bf16[8,7168]{1,0:T(8,128)(2,1)}, u32[]{:S(2)}) copy-start(bf16[8,7168]{1,0:T(8,128)(2,1)} %param.19) | copy-start | bytes 344068
  112.1 111.1 %copy-start.7 = (f32[7168]{0:T(1024)S(1)}, f32[7168]{0:T(1024)}, u32[]{:S(2)}) copy-start(f32[7168]{0:T(1024)} %param.20) | copy-start | bytes 86020
  112.2 177.6 %all-gather.5.cloned.1.call-start = ((), (), s32[]{:S(2)}) async-start(), calls=%async_computation.4 | async-start | bytes 7798784 | tf_op jit(solution)/shard_map/all_gather | solution.py:167
  239.8 146.4 %reduce-scatter.2.cloned.1.call-start = ((), (), s32[]{:S(2)}) async-start(), calls=%async_computation.5 | async-start | bytes 7798784 | tf_op jit(solution)/shard_map/reduce_scatter | solution.py:175
  305.2 5.8 %copy-start.1 = (bf16[512,7168]{1,0:T(8,128)(2,1)S(1)}, bf16[512,7168]{1,0:T(8,128)(2,1)}, u32[]{:S(2)}) copy-start(bf16[512,7168]{1,0:T(8,128)(2,1)} %reshape.232) | copy-start | bytes 22020100
  305.2 6.2 %copy-start.13 = (bf16[1,7168,128]{2,1,0:T(8,128)(2,1)S(1)}, bf16[1,7168,128]{2,1,0:T(8,128)(2,1)}, u32[]{:S(2)}) copy-start(bf16[1,7168,128]{2,1,0:T(8,128)(2,1)} %param.24) | copy-start | bytes 5505028
  318.4 77.4 %copy-start.12 = (f32[8,2]{0,1:T(2,128)S(1)}, f32[8,2]{0,1:T(2,128)}, u32[]{:S(2)}) copy-start(f32[8,2]{0,1:T(2,128)} %param.22) | copy-start | bytes 196
  388.6 15.6 %all-to-all-start.1 = ((bf16[16,2,7168]{2,1,0:T(2,128)(2,1)}), bf16[16,2,7168]{2,1,0:T(2,128)(2,1)S(1)}, u32[]{:S(2)}, u32[]{:S(2)}) async-start(bf16[16,2,7168]{2,1,0:T(2,128)(2,1)} %copy.99), calls=%async_computation.2 | async-start | bytes 917504 | tf_op jit(solution)/shard_map/all_to_all | solution.py:178
Sparse Core Ops, SparseCore 0:
  9.2 68.1 all-gather.2
  112.3 109.8 all-reduce.2
  240.0 49.7 all-gather.4
  318.6 67.6 reduce-scatter.1
where the time goes:
time: 414 us; the launch traced here: 413 us
  waiting for transfers between devices  243 us (59%)
  blocking collectives  52.3 us (13%)
  starting transfers between devices  37.2 us (9%)
  local copies, waits for them, and re-layouts  31.5 us (8%)
  matrix products  29.6 us (7%)
  between operations  14.3 us (3%)
  other arithmetic  5.39 us (1%)
    unnamed x5, waiting for transfers between devices  108 us
    reduce_scatter x1, waiting for transfers between devices, local(): lax.psum_scatter(partial_out.astype(jnp.bfloat16), 'ctx', scatter_dimensi...  67.8 us
    all_gather x1, waiting for transfers between devices, local(): portion = lax.all_gather(arrived, 'ctx', axis=0, tiled=True)  49.7 us
    ppermute x10, starting transfers between devices, passed_along(): return lax.ppermute(block, axis, route)  29.6 us
    all_gather x1, blocking collectives, local(): part_values = lax.all_gather(comp_values, 'ctx', axis=0, tiled=True)  19 us
    all_gather x1, blocking collectives, local(): part_keys = lax.all_gather(comp_keys, 'ctx', axis=0, tiled=True)  18.2 us
    reshape x1, local copies, waits for them, and re-layouts, local(): flat_rows = portion.reshape(-1, model_width)  15.4 us
    all_to_all x1, blocking collectives, local(): lax.all_to_all(outgoing, 'exp', split_axis=0, concat_axis=0, tiled=True)  15.1 us
  transfers between devices with their start and end apart: 15, of which 6 were waited for; matrix products, arithmetic and copies ran while one was open for 6% of the time, Pallas kernels for 0%

commit v1 on v0

--- a/solution.py
+++ b/solution.py
@@ -7,6 +7,12 @@
 WINDOW = 512
 score_gain = 2.0
 norm_eps = 1e-06
+
+
+def _review_gates(message, field):
+    earlier = jnp.concatenate([message, field], 1)
+    val = lax.all_gather(earlier, "ctx", tiled=True, axis=0)
+    return jnp.split(val, [message.shape[1]], 1)
 
 
 def passed_along(block, axis, distance):
@@ -71,8 +77,7 @@
     ).astype(jnp.bfloat16)
     query_pos = ctx_index * row_count + jnp.arange(row_count, dtype=jnp.int32)
     query_heads = query_norm.reshape(row_count, head_count, head_width)
-    part_keys = lax.all_gather(comp_keys, "ctx", axis=0, tiled=True)
-    part_values = lax.all_gather(comp_values, "ctx", axis=0, tiled=True)
+    part_keys, part_values = _review_gates(comp_keys, comp_values)
     part_count = part_keys.shape[0]
     scores = jnp.einsum(
         "thd,nhd->htn",

time: 414 us -> 400 us (0.966)
  blocking collectives: 52.3 us -> 35.7 us
    all_gather x2 -> x1, blocking collectives: 37.3 us -> 20.7 us  [_review_gates(): val = lax.all_gather(earlier, 'ctx', tiled=True, axis=0)]
  transfers between devices with their start and end apart: 15 -> 15, of which waited for: 6 -> 7; matrix products, arithmetic and copies ran while one was open for 6% -> 6% of each run, Pallas kernels for 0% -> 0%
where the time goes in v1:
time: 400 us; the launch traced here: 399 us
  waiting for transfers between devices  243 us (61%)
  starting transfers between devices  38.7 us (10%)
  blocking collectives  35.7 us (9%)
  local copies, waits for them, and re-layouts  31.9 us (8%)
  matrix products  28.4 us (7%)
  between operations  14.3 us (4%)
  other arithmetic  7.15 us (2%)
    unnamed x5, waiting for transfers between devices  108 us
    reduce_scatter x1, waiting for transfers between devices, local(): lax.psum_scatter(partial_out.astype(jnp.bfloat16), 'ctx', scatter_dimensi...  67.8 us
    all_gather x1, waiting for transfers between devices, local(): portion = lax.all_gather(arrived, 'ctx', axis=0, tiled=True)  49.7 us
    ppermute x10, starting transfers between devices, passed_along(): return lax.ppermute(block, axis, route)  31.1 us
    all_gather x1, blocking collectives, _review_gates(): val = lax.all_gather(earlier, 'ctx', tiled=True, axis=0)  20.7 us
    reshape x1, local copies, waits for them, and re-layouts, local(): flat_rows = portion.reshape(-1, model_width)  15.4 us
    all_to_all x1, blocking collectives, local(): lax.all_to_all(outgoing, 'exp', split_axis=0, concat_axis=0, tiled=True)  15.1 us
    ppermute x10, waiting for transfers between devices, passed_along(): return lax.ppermute(block, axis, route)  9.42 us
  transfers between devices with their start and end apart: 15, of which 7 were waited for; matrix products, arithmetic and copies ran while one was open for 6% of the time, Pallas kernels for 0%

profile of v1, /device:TPU:8, one launch (start us, length us, event | category | flops | bytes accessed | tf_op | source)
XLA Modules:
  0.0 399.2 jit_solution(6699624199861168681)
XLA Ops:
  8.4 5.2 %collective-permute-start.6 = (bf16[128,512]{0,1:T(8,128)(2,1)S(1)}, bf16[128,512]{0,1:T(8,128)(2,1)S(1)}, u32[]{:S(2)}, u32[]{:S(2)}) collective-permute-start(bf16[128,512]{0,1:T(8,128)(2,1)S(1)} %fusion.24), channel_id=1, source_target_pairs={{0,64},{16,80},{32,96},{48,112},{64,128},{80,144},{96,160},{112,17... | collective-permute-start | bytes 393224 | tf_op jit(solution)/shard_map/ppermute | solution.py:21
  13.6 3.0 collective-permute-start.7
  16.6 5.7 %collective-permute-start.8 = (bf16[128,512]{0,1:T(8,128)(2,1)S(1)}, bf16[128,512]{0,1:T(8,128)(2,1)}, u32[]{:S(2)}, u32[]{:S(2)}) collective-permute-start(bf16[128,512]{0,1:T(8,128)(2,1)S(1)} %fusion.24), channel_id=1, source_target_pairs={{0,32},{16,48},{32,64},{48,80},{64,96},{80,112},{96,128},{112,144}... | collective-permute-start | bytes 393224 | tf_op jit(solution)/shard_map/ppermute | solution.py:21
  22.3 2.7 collective-permute-start.2
  25.1 1.3 slice.66
  26.4 1.3 collective-permute-start
  32.2 1.4 fusion.50
  37.0 3.7 collective-permute-start.3
  41.1 2.8 collective-permute-start.4
  43.9 3.4 collective-permute-done.3
  47.3 2.5 collective-permute-start.5
  49.9 3.1 collective-permute-done.4
  52.9 3.0 collective-permute-start.9
  56.0 1.3 collective-permute-start.1
  57.3 2.9 collective-permute-done.1
  61.2 20.7 %all_gather.9 = bf16[128,1024]{1,0:T(8,128)(2,1)S(1)} all-gather(bf16[8,1024]{1,0:T(8,128)(2,1)S(1)} %pad_maximum_fusion.2), channel_id=1, replica_groups=mesh['ctx'=16,'exp'=16] {'ctx'}, dimensions={0}, use_global_device_ids=true | all-gather | bytes 278528 | tf_op jit(solution)/shard_map/all_gather | solution.py:14
  83.4 1.6 constant_dynamic-update-slice_fusion.7
  85.0 1.6 constant_dynamic-update-slice_fusion.6
  89.1 1.7 fusion.51
  91.4 7.5 %fusion.53 = f32[128,7168]{1,0:T(8,128)} fusion(bf16[128,512]{0,1:T(8,128)(2,1)S(1)} %bitcast.126, bf16[512,7168]{0,1:T(8,128)(2,1)} %all-gather.3.cloned.1.call-done), kind=kOutput, calls=%fused_computation.103 | convolution fusion | flops 939524096 | bytes 11141120 | tf_op jit(solution)/shard_map/dot_general | solution.py:141
  101.5 107.0 %all-reduce.3.cloned.1.call-done = f32[128,7168]{1,0:T(8,128)} async-done(((f32[128,7168]{1,0:T(8,128)}), f32[128,7168]{1,0:T(8,128)}) %all-reduce.3.cloned.1.call-update) | async-done | bytes 3670032
  211.1 15.1 %all_to_all.10 = bf16[16,2,7168]{2,1,0:T(2,128)(2,1)} all-to-all(bf16[16,2,7168]{2,1,0:T(2,128)(2,1)S(1)} %reshape.231), channel_id=1, replica_groups=mesh['ctx'=16,'exp'=16] {'exp'}, dimensions={0} | all-to-all | bytes 917504 | tf_op jit(solution)/shard_map/all_to_all | solution.py:168
  226.5 49.7 %all-gather.5.cloned.1.call-done = bf16[256,2,7168]{2,1,0:T(2,128)(2,1)} async-done(((bf16[16,2,7168]{2,1,0:T(2,128)(2,1)}), bf16[256,2,7168]{2,1,0:T(2,128)(2,1)}) %all-gather.5.cloned.1.call-update) | async-done | bytes 7340048 | tf_op jit(solution)/shard_map/all_gather | solution.py:172
  276.1 15.4 %reshape.232 = bf16[512,7168]{1,0:T(8,128)(2,1)} reshape(bf16[256,2,7168]{2,1,0:T(2,128)(2,1)} %all-gather.5.cloned.1.call-done) | data formatting | bytes 14680064 | tf_op jit(solution)/shard_map/reshape | solution.py:173
  291.5 5.8 %fusion.4 = f32[512,128]{1,0:T(8,128)S(1)} fusion(bf16[512,7168]{1,0:T(8,128)(2,1)} %reshape.232, bf16[1,7168,128]{2,1,0:T(8,128)(2,1)} %param.23), kind=kOutput, calls=%fused_computation.7 | convolution fusion | flops 939524096 | bytes 9437184 | tf_op jit(solution)/shard_map/dot_general | solution.py:174
  297.7 2.1 fusion.19
  299.8 5.0 %convolution_convert_fusion = bf16[256,2,7168]{2,0,1:T(8,128)(2,1)} fusion(bf16[1,128,7168]{2,1,0:T(8,128)(2,1)S(1)} %copy-done, bf16[256,2,128]{2,1,0:T(2,128)(2,1)S(1)} %bitcast.127), kind=kOutput, calls=%fused_computation | convolution fusion | flops 943194112 | bytes 9306112 | tf_op jit(solution)/shard_map/dot_general | solution.py:177
  304.8 67.8 %reduce-scatter.2.cloned.1.call-done = bf16[16,2,7168]{2,0,1:T(8,128)(2,1)} async-done(((bf16[256,2,7168]{2,0,1:T(8,128)(2,1)}), bf16[16,2,7168]{2,0,1:T(8,128)(2,1)}) %reduce-scatter.2.cloned.1.call-update) | async-done | bytes 458768 | tf_op jit(solution)/shard_map/reduce_scatter | solution.py:180
  372.7 2.3 copy.99
  374.9 7.3 %all-to-all-start.1 = ((bf16[16,2,7168]{2,1,0:T(2,128)(2,1)}), bf16[16,2,7168]{2,1,0:T(2,128)(2,1)S(1)}, u32[]{:S(2)}, u32[]{:S(2)}) async-start(bf16[16,2,7168]{2,1,0:T(2,128)(2,1)} %copy.99), calls=%async_computation.2 | async-start | bytes 917504 | tf_op jit(solution)/shard_map/all_to_all | solution.py:183
  382.3 8.3 %all-to-all-done.1 = bf16[16,2,7168]{2,1,0:T(2,128)(2,1)S(1)} async-done(((bf16[16,2,7168]{2,1,0:T(2,128)(2,1)}), bf16[16,2,7168]{2,1,0:T(2,128)(2,1)S(1)}, u32[]{:S(2)}, u32[]{:S(2)}) %all-to-all-start.1) | async-done | bytes 458784 | tf_op jit(solution)/shard_map/all_to_all | solution.py:183
  390.8 1.9 fusion
  (110 shorter events, 21.0 us)
Async XLA Ops:
  6.5 293.3 %copy-start = (bf16[1,128,7168]{2,1,0:T(8,128)(2,1)S(1)}, bf16[1,128,7168]{2,1,0:T(8,128)(2,1)}, u32[]{:S(2)}) copy-start(bf16[1,128,7168]{2,1,0:T(8,128)(2,1)} %param.25) | copy-start | bytes 5505028
  6.5 34.1 %copy-start.2 = (bf16[128,512]{1,0:T(8,128)(2,1)S(1)}, bf16[128,512]{1,0:T(8,128)(2,1)}, u32[]{:S(2)}) copy-start(bf16[128,512]{1,0:T(8,128)(2,1)} %param.14) | copy-start | bytes 393220
  6.5 30.4 %copy-start.4 = (bf16[128,512]{1,0:T(8,128)(2,1)S(1)}, bf16[128,512]{1,0:T(8,128)(2,1)}, u32[]{:S(2)}) copy-start(bf16[128,512]{1,0:T(8,128)(2,1)} %param.15) | copy-start | bytes 393220
  6.5 29.2 %copy-start.5 = (bf16[128,512]{1,0:T(8,128)(2,1)S(1)}, bf16[128,512]{1,0:T(8,128)(2,1)}, u32[]{:S(2)}) copy-start(bf16[128,512]{1,0:T(8,128)(2,1)} %param.13) | copy-start | bytes 393220
  6.5 84.8 %all-gather.3.cloned.1.call-start = ((), (), s32[]{:S(2)}) async-start(), calls=%async_computation.3 | async-start | bytes 7798784 | tf_op jit(solution)/shard_map/all_gather | solution.py:143
  7.3 201.3 %all-reduce.3.cloned.1.call-start = ((), (), s32[]{:S(2)}) async-start(), calls=%async_computation.6 | async-start | bytes 7340032
  8.4 73.4 %collective-permute-start.6 = (bf16[128,512]{0,1:T(8,128)(2,1)S(1)}, bf16[128,512]{0,1:T(8,128)(2,1)S(1)}, u32[]{:S(2)}, u32[]{:S(2)}) collective-permute-start(bf16[128,512]{0,1:T(8,128)(2,1)S(1)} %fusion.24), channel_id=1, source_target_pairs={{0,64},{16,80},{32,96},{48,112},{64,128},{80,144},{96,160},{112,17... | collective-permute-start | bytes 393224 | tf_op jit(solution)/shard_map/ppermute | solution.py:21
  13.6 68.3 %collective-permute-start.7 = (bf16[128,512]{0,1:T(8,128)(2,1)S(1)}, bf16[128,512]{0,1:T(8,128)(2,1)S(1)}, u32[]{:S(2)}, u32[]{:S(2)}) collective-permute-start(bf16[128,512]{0,1:T(8,128)(2,1)S(1)} %fusion.24), channel_id=1, source_target_pairs={{0,48},{16,64},{32,80},{48,96},{64,112},{80,128},{96,144},{112,160... | collective-permute-start | bytes 393224 | tf_op jit(solution)/shard_map/ppermute | solution.py:21
  16.6 66.7 %collective-permute-start.8 = (bf16[128,512]{0,1:T(8,128)(2,1)S(1)}, bf16[128,512]{0,1:T(8,128)(2,1)}, u32[]{:S(2)}, u32[]{:S(2)}) collective-permute-start(bf16[128,512]{0,1:T(8,128)(2,1)S(1)} %fusion.24), channel_id=1, source_target_pairs={{0,32},{16,48},{32,64},{48,80},{64,96},{80,112},{96,128},{112,144}... | collective-permute-start | bytes 393224 | tf_op jit(solution)/shard_map/ppermute | solution.py:21
  22.3 18.8 %collective-permute-start.2 = (bf16[128,512]{1,0:T(8,128)(2,1)}, bf16[128,512]{1,0:T(8,128)(2,1)S(1)}, u32[]{:S(2)}, u32[]{:S(2)}) collective-permute-start(bf16[128,512]{1,0:T(8,128)(2,1)} %param.15), channel_id=1, source_target_pairs={{0,64},{16,80},{32,96},{48,112},{64,128},{80,144},{96,160},{112,17... | collective-permute-start | bytes 393224 | tf_op jit(solution)/shard_map/ppermute | solution.py:21
  26.4 10.6 %collective-permute-start = (bf16[16,512]{1,0:T(8,128)(2,1)}, bf16[16,512]{1,0:T(8,128)(2,1)S(1)}, u32[]{:S(2)}, u32[]{:S(2)}) collective-permute-start(bf16[16,512]{1,0:T(8,128)(2,1)} %slice.66), channel_id=1, source_target_pairs={{16,0},{32,16},{48,32},{64,48},{80,64},{96,80},{112,96},{128,112},... | collective-permute-start | bytes 49160 | tf_op jit(solution)/shard_map/ppermute | solution.py:21
  37.0 10.3 %collective-permute-start.3 = (bf16[128,512]{1,0:T(8,128)(2,1)S(1)}, bf16[128,512]{1,0:T(8,128)(2,1)S(1)}, u32[]{:S(2)}, u32[]{:S(2)}) collective-permute-start(bf16[128,512]{1,0:T(8,128)(2,1)S(1)} %copy-done.4), channel_id=1, source_target_pairs={{0,48},{16,64},{32,80},{48,96},{64,112},{80,128},{96,144},{112,160... | collective-permute-start | bytes 393224 | tf_op jit(solution)/shard_map/ppermute | solution.py:21
  41.1 11.8 %collective-permute-start.4 = (bf16[128,512]{1,0:T(8,128)(2,1)S(1)}, bf16[128,512]{1,0:T(8,128)(2,1)S(1)}, u32[]{:S(2)}, u32[]{:S(2)}) collective-permute-start(bf16[128,512]{1,0:T(8,128)(2,1)S(1)} %copy-done.4), channel_id=1, source_target_pairs={{0,32},{16,48},{32,64},{48,80},{64,96},{80,112},{96,128},{112,144}... | collective-permute-start | bytes 393224 | tf_op jit(solution)/shard_map/ppermute | solution.py:21
  47.3 8.7 %collective-permute-start.5 = (bf16[128,512]{1,0:T(8,128)(2,1)S(1)}, bf16[128,512]{1,0:T(8,128)(2,1)S(1)}, u32[]{:S(2)}, u32[]{:S(2)}) collective-permute-start(bf16[128,512]{1,0:T(8,128)(2,1)S(1)} %copy-done.4), channel_id=1, source_target_pairs={{0,16},{16,32},{32,48},{48,64},{64,80},{80,96},{96,112},{112,128},... | collective-permute-start | bytes 393224 | tf_op jit(solution)/shard_map/ppermute | solution.py:21
  52.9 32.0 %collective-permute-start.9 = (bf16[128,512]{0,1:T(8,128)(2,1)S(1)}, bf16[128,512]{0,1:T(8,128)(2,1)}, u32[]{:S(2)}, u32[]{:S(2)}) collective-permute-start(bf16[128,512]{0,1:T(8,128)(2,1)S(1)} %fusion.24), channel_id=1, source_target_pairs={{0,16},{16,32},{32,48},{48,64},{64,80},{80,96},{96,112},{112,128},... | collective-permute-start | bytes 393224 | tf_op jit(solution)/shard_map/ppermute | solution.py:21
  56.0 4.2 %collective-permute-start.1 = (bf16[16,512]{1,0:T(8,128)(2,1)S(1)}, bf16[16,512]{1,0:T(8,128)(2,1)S(1)}, u32[]{:S(2)}, u32[]{:S(2)}) collective-permute-start(bf16[16,512]{1,0:T(8,128)(2,1)S(1)} %slice.74), channel_id=1, source_target_pairs={{16,0},{32,16},{48,32},{64,48},{80,64},{96,80},{112,96},{128,112},... | collective-permute-start | bytes 49160 | tf_op jit(solution)/shard_map/ppermute | solution.py:21
  60.2 30.5 %copy-start.9 = (f32[128,4]{0,1:T(4,128)S(1)}, f32[128,4]{0,1:T(4,128)}, u32[]{:S(2)}) copy-start(f32[128,4]{0,1:T(4,128)} %get-tuple-element.10) | copy-start | bytes 6148
  82.0 0.8 copy-start.7
  82.8 8.4 %copy-start.8 = (f32[128,4]{0,1:T(4,128)S(1)}, f32[128,4]{0,1:T(4,128)}, u32[]{:S(2)}) copy-start(f32[128,4]{0,1:T(4,128)} %get-tuple-element.9) | copy-start | bytes 6148
  98.9 0.7 copy-start.10
  98.9 1.3 copy-start.13
  98.9 109.6 %copy-start.3 = (bf16[8,7168]{1,0:T(8,128)(2,1)S(1)}, bf16[8,7168]{1,0:T(8,128)(2,1)}, u32[]{:S(2)}) copy-start(bf16[8,7168]{1,0:T(8,128)(2,1)} %param.19) | copy-start | bytes 344068
  98.9 110.8 %copy-start.6 = (f32[7168]{0:T(1024)S(1)}, f32[7168]{0:T(1024)}, u32[]{:S(2)}) copy-start(f32[7168]{0:T(1024)} %param.20) | copy-start | bytes 86020
  98.9 177.2 %all-gather.5.cloned.1.call-start = ((), (), s32[]{:S(2)}) async-start(), calls=%async_computation.4 | async-start | bytes 7798784 | tf_op jit(solution)/shard_map/all_gather | solution.py:172
  226.2 146.4 %reduce-scatter.2.cloned.1.call-start = ((), (), s32[]{:S(2)}) async-start(), calls=%async_computation.5 | async-start | bytes 7798784 | tf_op jit(solution)/shard_map/reduce_scatter | solution.py:180
  291.5 5.8 %copy-start.1 = (bf16[512,7168]{1,0:T(8,128)(2,1)S(1)}, bf16[512,7168]{1,0:T(8,128)(2,1)}, u32[]{:S(2)}) copy-start(bf16[512,7168]{1,0:T(8,128)(2,1)} %reshape.232) | copy-start | bytes 22020100
  291.5 6.2 %copy-start.12 = (bf16[1,7168,128]{2,1,0:T(8,128)(2,1)S(1)}, bf16[1,7168,128]{2,1,0:T(8,128)(2,1)}, u32[]{:S(2)}) copy-start(bf16[1,7168,128]{2,1,0:T(8,128)(2,1)} %param.24) | copy-start | bytes 5505028
  304.8 77.4 %copy-start.11 = (f32[8,2]{0,1:T(2,128)S(1)}, f32[8,2]{0,1:T(2,128)}, u32[]{:S(2)}) copy-start(f32[8,2]{0,1:T(2,128)} %param.22) | copy-start | bytes 196
  374.9 15.6 %all-to-all-start.1 = ((bf16[16,2,7168]{2,1,0:T(2,128)(2,1)}), bf16[16,2,7168]{2,1,0:T(2,128)(2,1)S(1)}, u32[]{:S(2)}, u32[]{:S(2)}) async-start(bf16[16,2,7168]{2,1,0:T(2,128)(2,1)} %copy.99), calls=%async_computation.2 | async-start | bytes 917504 | tf_op jit(solution)/shard_map/all_to_all | solution.py:183
Sparse Core Ops, SparseCore 0:
  9.2 71.2 all-gather.2
  99.1 109.4 all-reduce.2
  226.3 49.7 all-gather.4
  305.0 67.6 reduce-scatter.1
